TPU v7x, 32 devices: a whole 2x2x4 slice. The times are simulated.
32 devices in a mesh: dp: 16 (over z, y, core), tensor: 2 (over x).
Axes of the slice: x: 2, y: 2, z: 4, core: 2. Of those that a mesh axis runs over, the one named last changes fastest.
Arguments:
- tokens: bfloat16 [25088, 512], P(('dp', 'tensor')), may hold values from -6 to 6
- cotangent: bfloat16 [25088, 512], P(('dp', 'tensor')), may hold values from -6 to 6
- ln1_scale: float32 [512], P(('dp', 'tensor')), may hold values from 0.5 to 1.5
- ln1_shift: float32 [512], P(('dp', 'tensor')), may hold values from -1.75 to 1.75
- w_qkv: float32 [3, 512, 512], P(None, ('dp', 'tensor')), may hold values from -0.375 to 0.375
- w_out: float32 [512, 512], P(('dp', 'tensor')), may hold values from -0.75 to 0.75
- out_bias: float32 [512], P(('dp', 'tensor')), may hold values from -0.625 to 0.625
- ln2_scale: float32 [512], P(('dp', 'tensor')), may hold values from 0.5 to 1.5
- ln2_shift: float32 [512], P(('dp', 'tensor')), may hold values from -1.75 to 1.75
- w_router: float32 [512, 32], P(('dp', 'tensor')), may hold values from -0.1875 to 0.1875
- w_in: float32 [32, 512, 2048], P(None, 'dp', 'tensor'), may hold values from -0.25 to 0.25
- b_in: float32 [32, 2048], P('dp', 'tensor'), may hold values from -0.625 to 0.625
- w_back: float32 [32, 2048, 512], P(None, 'tensor', 'dp'), may hold values from -1.5 to 1.5
- b_back: float32 [32, 512], P(None, ('dp', 'tensor')), may hold values from -1.25 to 1.25
- choices: int32 [25088, 2], P(('dp', 'tensor')), may hold values from 0 to 31, as said below
- slots: int32 [25088, 2], P(('dp', 'tensor')), may hold values from -1 to 64, as said below
Outputs:
- result: bfloat16 [25088, 512], P(('dp', 'tensor'))
- grad_tokens: float32 [25088, 512], P(('dp', 'tensor'))
- grad_ln1_scale: float32 [512], P(('dp', 'tensor'))
- grad_ln1_shift: float32 [512], P(('dp', 'tensor'))
- grad_w_qkv: float32 [3, 512, 512], P(None, ('dp', 'tensor'))
- grad_w_out: float32 [512, 512], P(('dp', 'tensor'))
- grad_out_bias: float32 [512], P(('dp', 'tensor'))
- grad_ln2_scale: float32 [512], P(('dp', 'tensor'))
- grad_ln2_shift: float32 [512], P(('dp', 'tensor'))
- grad_w_router: float32 [512, 32], P(('dp', 'tensor'))
- grad_w_in: float32 [32, 512, 2048], P(None, 'dp', 'tensor')
- grad_b_in: float32 [32, 2048], P('dp', 'tensor')
- grad_w_back: float32 [32, 2048, 512], P(None, 'tensor', 'dp')
- grad_b_back: float32 [32, 512], P(None, ('dp', 'tensor'))
Inputs may be any that keep to these rules, and one draw needn't show every extreme that they name: `choices`: each token names two different experts. slots[t, k] is the number of pairs of the same device and expert that come before pair (t, k), where all first choices of the device's 784 tokens in token order come before all its second choices; it is -1 where that number is 65 or more.
All inputs are finite; a program needn't handle non-finite values.
Results may differ from a plain program's by a relative error of at most 0.015.
The roundings to bfloat16 on the way count: a program that leaves them out, or rounds other values in their place, can miss the bound.
Values may be sent and summed in bfloat16 or wider, within the bound.
A program may use at most 320 MiB of HBM per device.

v0:
```python
import jax
import jax.numpy as jnp
from jax import lax
from jax.sharding import PartitionSpec as P

H = 8
HD = 64
SEQ = 196
CAP = 65


def norm_affine(values_in, gain_vec, shift_vec):
    center = values_in - jnp.mean(values_in, axis=-1, keepdims=True)
    spread = jnp.mean(center * center, axis=-1, keepdims=True)
    return center * lax.rsqrt(spread + 1e-06) * gain_vec + shift_vec


def per_device(
    tokens,
    cotangent,
    ln1_scale,
    ln1_shift,
    w_qkv,
    w_out,
    out_bias,
    ln2_scale,
    ln2_shift,
    w_router,
    w_in,
    b_in,
    w_back,
    b_back,
    choices,
    slots,
):
    low_type = jnp.bfloat16
    wide_type = jnp.float32
    dense_set = (
        lax.all_gather(ln1_scale.astype(low_type), ("dp", "tensor"), axis=0, tiled=True),
        lax.all_gather(ln1_shift.astype(low_type), ("dp", "tensor"), axis=0, tiled=True),
        lax.all_gather(out_bias.astype(low_type), ("dp", "tensor"), axis=0, tiled=True),
        lax.all_gather(ln2_scale.astype(low_type), ("dp", "tensor"), axis=0, tiled=True),
        lax.all_gather(ln2_shift.astype(low_type), ("dp", "tensor"), axis=0, tiled=True),
        lax.all_gather(w_router.astype(low_type), ("dp", "tensor"), axis=0, tiled=True),
        lax.all_gather(b_back.astype(low_type), ("dp", "tensor"), axis=1, tiled=True),
        lax.all_gather(w_qkv.astype(low_type), ("dp", "tensor"), axis=1, tiled=True),
        lax.all_gather(w_out.astype(low_type), ("dp", "tensor"), axis=0, tiled=True),
    )
    gain_one = dense_set[0].astype(wide_type)
    shift_one = dense_set[1].astype(wide_type)
    bias_attn = dense_set[2].astype(wide_type)
    gain_two = dense_set[3].astype(wide_type)
    shift_two = dense_set[4].astype(wide_type)
    router = dense_set[5]
    bias_back = dense_set[6].astype(wide_type)
    qkv_w = dense_set[7]
    out_w = dense_set[8]
    in_w, in_b, back_w = (
        lax.all_gather(w_in.astype(low_type), "dp", axis=1, tiled=True),
        lax.all_gather(b_in.astype(low_type), "dp", axis=0, tiled=True),
        lax.all_gather(w_back.astype(low_type), "dp", axis=2, tiled=True),
    )
    rows_here = tokens.shape[0]
    model_width = tokens.shape[1]
    images = rows_here // SEQ
    experts = in_b.shape[0]
    slot_total = experts * CAP
    score_scale = HD ** (-0.5)
    residual = tokens.astype(wide_type)
    normed_one = norm_affine(residual, gain_one, shift_one).astype(low_type)
    projected = jnp.einsum(
        "td,jde->jte", normed_one, qkv_w, preferred_element_type=wide_type
    ).astype(low_type)
    head_query = projected[0].reshape(images, SEQ, H, HD)
    head_key = projected[1].reshape(images, SEQ, H, HD)
    head_value = projected[2].reshape(images, SEQ, H, HD)
    raw_scores = jnp.einsum(
        "ishd,ithd->ihst", head_query, head_key, preferred_element_type=wide_type
    )
    scaled = raw_scores * score_scale
    row_top = jnp.max(scaled, axis=-1, keepdims=True)
    log_total = row_top + jnp.log(jnp.sum(jnp.exp(scaled - row_top), axis=-1, keepdims=True))
    weights_att = jnp.exp(scaled - log_total).astype(low_type)
    attended = (
        jnp.einsum("ihst,ithd->ishd", weights_att, head_value, preferred_element_type=wide_type)
        .astype(low_type)
        .reshape(rows_here, model_width)
    )
    attn_sum = jnp.dot(attended, out_w, preferred_element_type=wide_type)
    middle = residual + attn_sum + bias_attn
    normed_two = norm_affine(middle, gain_two, shift_two).astype(low_type)
    route_p = jax.nn.softmax(jnp.dot(normed_two, router, preferred_element_type=wide_type), axis=-1)
    gate_vals = jnp.take_along_axis(route_p, choices, axis=1)
    kept_pair = (slots >= 0).astype(wide_type)
    target = jnp.where(slots >= 0, choices * CAP + slots, -1)
    pair_target = target.reshape(-1)
    slot_match = pair_target[:, None] == jnp.arange(slot_total, dtype=jnp.int32)[None, :]
    source = jnp.max(
        jnp.where(slot_match, jnp.arange(2 * rows_here, dtype=jnp.int32)[:, None], -1), axis=0
    )
    filled = source >= 0
    source_safe = jnp.maximum(source, 0)
    source_tok = source_safe // 2
    buffer = jnp.where(filled[:, None], normed_two[source_tok], jnp.zeros((), low_type)).reshape(
        experts, CAP, model_width
    )
    first_b = in_b.astype(wide_type)
    all_slots = lax.all_gather(buffer, "tensor", axis=1, tiled=True)
    pre_act = (
        jnp.einsum("ecd,edf->ecf", all_slots, in_w, preferred_element_type=wide_type)
        + first_b[:, None, :]
    )
    hidden = jax.nn.gelu(pre_act, approximate=True).astype(low_type)
    partial_out = jnp.einsum("ecf,efd->ecd", hidden, back_w, preferred_element_type=wide_type)
    expert_sum = lax.psum_scatter(
        partial_out.astype(jnp.bfloat16), "tensor", scatter_dimension=1, tiled=True
    ).astype(jnp.float32)
    expert_out = (expert_sum + bias_back[:, None, :]).reshape(slot_total, model_width)
    index_safe = jnp.maximum(target, 0)
    picked = expert_out[index_safe]
    pair_weight = gate_vals * kept_pair
    result = (middle + jnp.sum(pair_weight[:, :, None] * picked, axis=1)).astype(low_type)
    grad_out = cotangent.astype(wide_type)
    pair_gate = pair_weight.reshape(-1)
    slot_grad = jnp.where(
        filled[:, None], pair_gate[source_safe][:, None] * grad_out[source_tok], 0.0
    )
    grad_bias_back = jnp.sum(slot_grad.reshape(experts, CAP, model_width), axis=1)
    slot_grad_low = slot_grad.astype(low_type).reshape(experts, CAP, model_width)
    slot_grad_all = lax.all_gather(slot_grad_low, "tensor", axis=1, tiled=True)
    grad_hidden = jnp.einsum(
        "ecd,efd->ecf", slot_grad_all, back_w, preferred_element_type=wide_type
    )
    grad_second = jnp.einsum(
        "ecf,ecd->efd", hidden, slot_grad_all, preferred_element_type=wide_type
    )
    gelu_value, gelu_pull = jax.vjp(lambda member: jax.nn.gelu(member, approximate=True), pre_act)
    grad_pre = gelu_pull(grad_hidden)[0].astype(low_type)
    grad_first_b = jnp.sum(grad_pre.astype(wide_type), axis=1)
    grad_first_w = jnp.einsum("ecd,ecf->edf", all_slots, grad_pre, preferred_element_type=wide_type)
    grad_slots_part = jnp.einsum("ecf,edf->ecd", grad_pre, in_w, preferred_element_type=wide_type)
    grad_slots = lax.psum_scatter(
        grad_slots_part.astype(jnp.bfloat16), "tensor", scatter_dimension=1, tiled=True
    ).astype(jnp.float32)
    expert_sums = (
        lax.psum_scatter(
            grad_first_w.astype(jnp.bfloat16), "dp", scatter_dimension=1, tiled=True
        ).astype(jnp.float32),
        lax.psum_scatter(
            grad_first_b.astype(jnp.bfloat16), "dp", scatter_dimension=0, tiled=True
        ).astype(jnp.float32),
        lax.psum_scatter(
            grad_second.astype(jnp.bfloat16), "dp", scatter_dimension=2, tiled=True
        ).astype(jnp.float32),
    )
    grad_slots = grad_slots.reshape(slot_total, model_width)
    grad_normed_two = jnp.sum(kept_pair[:, :, None] * grad_slots[index_safe], axis=1)
    gate_grad = kept_pair * jnp.sum(grad_out[:, None, :] * picked, axis=-1)
    expert_ids = jnp.arange(experts, dtype=jnp.int32)
    grad_probs = jnp.sum(
        gate_grad[:, :, None]
        * (choices[:, :, None] == expert_ids[None, None, :]).astype(wide_type),
        axis=1,
    )
    grad_logits = route_p * (grad_probs - jnp.sum(grad_probs * route_p, axis=-1, keepdims=True))
    router_wide = router.astype(wide_type)
    grad_normed_two = grad_normed_two + jnp.dot(
        grad_logits, router_wide.T, precision=lax.Precision.HIGHEST
    )
    grad_router = jnp.dot(
        normed_two.astype(wide_type).T, grad_logits, precision=lax.Precision.HIGHEST
    )
    norm_two_value, pull_two = jax.vjp(norm_affine, middle, gain_two, shift_two)
    grad_mid_norm, grad_gain_two, grad_shift_two = pull_two(grad_normed_two)
    grad_middle = grad_out + grad_mid_norm
    grad_bias_attn = jnp.sum(grad_middle, axis=0)
    grad_mid_low = grad_middle.astype(low_type)
    grad_att = jnp.einsum(
        "td,ed->te", grad_mid_low, out_w, preferred_element_type=wide_type
    ).astype(low_type)
    grad_out_w = jnp.einsum("te,td->ed", attended, grad_mid_low, preferred_element_type=wide_type)
    grad_att_heads = grad_att.reshape(images, SEQ, H, HD)
    probs_again = jnp.exp(
        jnp.einsum("ishd,ithd->ihst", head_query, head_key, preferred_element_type=wide_type)
        * score_scale
        - log_total
    )
    grad_weights = jnp.einsum(
        "ishd,ithd->ihst", grad_att_heads, head_value, preferred_element_type=wide_type
    )
    row_delta = jnp.sum(grad_weights * probs_again, axis=-1, keepdims=True)
    grad_raw = (probs_again * (grad_weights - row_delta) * score_scale).astype(low_type)
    grad_value = jnp.einsum(
        "ihst,ishd->ithd",
        probs_again.astype(low_type),
        grad_att_heads,
        preferred_element_type=wide_type,
    )
    grad_query = jnp.einsum("ihst,ithd->ishd", grad_raw, head_key, preferred_element_type=wide_type)
    grad_key = jnp.einsum("ihst,ishd->ithd", grad_raw, head_query, preferred_element_type=wide_type)
    grad_proj = jnp.stack(
        [
            grad_query.astype(low_type).reshape(rows_here, model_width),
            grad_key.astype(low_type).reshape(rows_here, model_width),
            grad_value.astype(low_type).reshape(rows_here, model_width),
        ]
    )
    grad_qkv_w = jnp.einsum("td,jte->jde", normed_one, grad_proj, preferred_element_type=wide_type)
    grad_normed_one = jnp.einsum("jte,jde->td", grad_proj, qkv_w, preferred_element_type=wide_type)
    norm_one_value, pull_one = jax.vjp(norm_affine, residual, gain_one, shift_one)
    grad_resid_norm, grad_gain_one, grad_shift_one = pull_one(grad_normed_one)
    grad_tokens = grad_middle + grad_resid_norm
    dense_sums = (
        lax.psum_scatter(grad_gain_one, ("dp", "tensor"), scatter_dimension=0, tiled=True),
        lax.psum_scatter(grad_shift_one, ("dp", "tensor"), scatter_dimension=0, tiled=True),
        lax.psum_scatter(grad_bias_attn, ("dp", "tensor"), scatter_dimension=0, tiled=True),
        lax.psum_scatter(grad_gain_two, ("dp", "tensor"), scatter_dimension=0, tiled=True),
        lax.psum_scatter(grad_shift_two, ("dp", "tensor"), scatter_dimension=0, tiled=True),
        lax.psum_scatter(grad_router, ("dp", "tensor"), scatter_dimension=0, tiled=True),
        lax.psum_scatter(grad_bias_back, ("dp", "tensor"), scatter_dimension=1, tiled=True),
        lax.psum_scatter(grad_qkv_w, ("dp", "tensor"), scatter_dimension=1, tiled=True),
        lax.psum_scatter(grad_out_w, ("dp", "tensor"), scatter_dimension=0, tiled=True),
    )
    return (
        result,
        grad_tokens,
        dense_sums[0],
        dense_sums[1],
        dense_sums[7],
        dense_sums[8],
        dense_sums[2],
        dense_sums[3],
        dense_sums[4],
        dense_sums[5],
        expert_sums[0],
        expert_sums[1],
        expert_sums[2],
        dense_sums[6],
    )


def solution(mesh):
    in_specs = (
        P(("dp", "tensor"), None),
        P(("dp", "tensor"), None),
        P(("dp", "tensor")),
        P(("dp", "tensor")),
        P(None, ("dp", "tensor"), None),
        P(("dp", "tensor"), None),
        P(("dp", "tensor")),
        P(("dp", "tensor")),
        P(("dp", "tensor")),
        P(("dp", "tensor"), None),
        P(None, "dp", "tensor"),
        P("dp", "tensor"),
        P(None, "tensor", "dp"),
        P(None, ("dp", "tensor")),
        P(("dp", "tensor"), None),
        P(("dp", "tensor"), None),
    )
    out_specs = (
        P(("dp", "tensor"), None),
        P(("dp", "tensor"), None),
        P(("dp", "tensor")),
        P(("dp", "tensor")),
        P(None, ("dp", "tensor"), None),
        P(("dp", "tensor"), None),
        P(("dp", "tensor")),
        P(("dp", "tensor")),
        P(("dp", "tensor")),
        P(("dp", "tensor"), None),
        P(None, "dp", "tensor"),
        P("dp", "tensor"),
        P(None, "tensor", "dp"),
        P(None, ("dp", "tensor")),
    )
    return jax.shard_map(
        per_device, mesh=mesh, in_specs=in_specs, out_specs=out_specs, check_vma=False
    )
```

profile of v0, /device:TPU:13, one launch (start us, length us, event | category | flops | bytes accessed | tf_op | source)
XLA Modules:
  0.0 2093.3 jit_solution(13447120301670424826)
XLA Ops:
  13.2 39.7 %all-reduce.13 = (bf16[512]{0:T(512)(128)(2,1)S(1)}, bf16[512]{0:T(512)(128)(2,1)S(1)}, bf16[512]{0:T(512)(128)(2,1)S(1)}, bf16[512]{0:T(512)(128)(2,1)S(1)}, bf16[512]{0:T(512)(128)(2,1)S(1)}) all-reduce(bf16[512]{0:T(512)(128)(2,1)S(1)} %dynamic-update-slice.1, ...), channel_id=1, replica_groups=mesh['dp'=16,'tensor'=2] {'dp','tensor'}, use_global_device_ids=true, to_apply=%add.1 | all-reduce | flops 2560 | bytes 10240
  55.5 2.2 select_reduce_fusion
  61.0 57.2 %all_gather.45 = bf16[512,512]{1,0:T(8,128)(2,1)} all-gather(bf16[16,512]{1,0:T(8,128)(2,1)S(1)} %convert_element_type.170), channel_id=1, replica_groups=mesh['dp'=16,'tensor'=2] {'dp','tensor'}, dimensions={0}, use_global_device_ids=true | all-gather | bytes 540672 | tf_op jit(solution)/shard_map/all_gather | solution.py:47
  118.2 3.2 convert_bitcast_fusion
  125.2 1.8 copy.320
  127.0 2.3 multiply_reduce_fusion.1
  129.3 2.7 copy-done.6
  135.3 4.6 fusion.55
  144.1 7.4 gather_fusion
  151.5 2.7 gather.25
  154.2 1.8 copy_select_fusion
  156.4 3.8 convert_element_type.179
  160.4 3.9 convert_element_type.183
  164.4 33.9 %all-gather = bf16[16,2,1024]{2,1,0:T(2,128)(2,1)S(1)} all-gather(bf16[1,2,1024]{2,1,0:T(2,128)(2,1)S(1)} %convert_bitcast_fusion.1), channel_id=1, replica_groups=mesh['dp'=16,'tensor'=2] {'dp'}, dimensions={0}, use_global_device_ids=true | all-gather | bytes 69632 | tf_op jit(solution)/shard_map/all_gather | solution.py:60
  199.6 6.8 gather_fusion.3
  206.5 5.0 gather.29
  211.5 49.5 %all_gather.49 = bf16[512,32]{1,0:T(8,128)(2,1)S(1)} all-gather(bf16[16,32]{1,0:T(8,128)(2,1)S(1)} %convert_element_type.178), channel_id=1, replica_groups=mesh['dp'=16,'tensor'=2] {'dp','tensor'}, dimensions={0}, use_global_device_ids=true | all-gather | bytes 33792 | tf_op jit(solution)/shard_map/all_gather | solution.py:44
  261.4 12.7 gather_fusion.5
  275.2 11.4 gather_fusion.2
  286.8 6.7 fusion.35
  293.6 103.8 %all-gather.11.cloned.1.call-done = bf16[32,512,1024]{2,1,0:T(8,128)(2,1)} async-done(((bf16[32,32,1024]{2,1,0:T(8,128)(2,1)}), bf16[32,512,1024]{2,1,0:T(8,128)(2,1)}) %all-gather.11.cloned.1.call-update) | async-done | bytes 33554448 | tf_op jit(solution)/shard_map/all_gather | solution.py:59
  397.4 23.7 %fusion.25 = f32[32,130,1024]{2,1,0:T(8,128)} fusion(bf16[32,512,1024]{2,1,0:T(8,128)(2,1)} %all-gather.11.cloned.1.call-done, bf16[32,130,512]{2,0,1:T(8,128)(2,1)} %all-gather.9.cloned.1.call-done), kind=kOutput, calls=%fused_computation.37 | convolution fusion | flops 4362076160 | bytes 54853632 | tf_op jit(solution)/shard_map/ecd,edf->ecf/dot_general | solution.py:110
  421.1 146.1 %all-gather.13.cloned.1.call-done = bf16[32,1024,512]{1,2,0:T(8,128)(2,1)} async-done(((bf16[32,1024,32]{1,2,0:T(8,128)(2,1)}), bf16[32,1024,512]{1,2,0:T(8,128)(2,1)}) %all-gather.13.cloned.1.call-update) | async-done | bytes 33554448 | tf_op jit(solution)/shard_map/all_gather | solution.py:61
  567.2 24.4 %convolution_convert_fusion.3 = bf16[32,130,512]{2,1,0:T(8,128)(2,1)} fusion(bf16[32,1024,512]{1,2,0:T(8,128)(2,1)} %all-gather.13.cloned.1.call-done, f32[32,130,1024]{2,1,0:T(8,128)} %fusion.25, f32[32,1024]{1,0:T(8,128)S(1)} %copy-done.35), kind=kOutput, calls=%fused_computation.49 | convolution fusion | flops 4406804480 | bytes 54984704 | tf_op jit(solution)/shard_map/ecf,efd->ecd/dot_general | solution.py:114
  591.6 5.7 copy.331
  597.5 28.9 %all-gather.15.cloned.1.call-done = bf16[32,130,512]{2,0,1:T(8,128)(2,1)} async-done(((bf16[32,65,512]{2,0,1:T(8,128)(2,1)}), bf16[32,130,512]{2,0,1:T(8,128)(2,1)}) %all-gather.15.cloned.1.call-update) | async-done | bytes 4259856 | tf_op jit(solution)/shard_map/all_gather | solution.py:130
  626.5 31.3 %fusion.94 = (bf16[32,1024]{1,0:T(8,128)(2,1)}, bf16[32,130,1024]{2,1,0:T(8,128)(2,1)}) fusion(f32[32,130,1024]{2,1,0:T(8,128)} %fusion.25, f32[32,1024]{1,0:T(8,128)S(1)} %copy-done.35, bf16[32,1024,512]{1,2,0:T(8,128)(2,1)} %all-gather.13.cloned.1.call-done, bf16[32,130,512]{2,0,1:T(8,128)(2,1)} %all-gather.15.cloned.1.call-done), kind=kOutput, calls=%fused_computation.151 | convolution fusion | flops 4455759872 | bytes 63569920 | tf_op jit(solution)/shard_map/ecd,efd->ecf/dot_general | solution.py:131
  657.8 20.2 convolution_convert_fusion.2
  678.0 5.8 copy.340
  684.5 50.4 %all_gather.54 = bf16[32,512]{0,1:T(8,128)(2,1)S(1)} all-gather(bf16[32,16]{0,1:T(8,128)(2,1)S(1)} %convert_element_type.186), channel_id=1, replica_groups=mesh['dp'=16,'tensor'=2] {'dp','tensor'}, dimensions={1}, use_global_device_ids=true | all-gather | bytes 33792 | tf_op jit(solution)/shard_map/all_gather | solution.py:45
  736.7 2.3 convert_add_fusion
  739.0 4.6 copy.333
  743.6 5.1 reshape.226
  748.7 8.5 gather_fusion.1
  757.2 5.3 reshape.242
  762.6 11.1 multiply_reduce_fusion.2
  774.0 5.0 copy.341
  779.0 5.1 reshape.232
  784.2 8.5 gather_fusion.4
  792.7 3.8 reshape.266
  796.6 18.2 multiply_reduce_fusion.3
  821.6 4.3 fusion.56
  825.9 3.8 fusion.95
  829.7 11.8 fusion.57
  841.5 12.8 fusion.60
  857.2 2.1 copy.369
  861.0 2.1 copy.368
  868.8 3.6 convolution_bitcast_fusion
  872.4 5.1 copy.358
  877.6 34.3 %convolution_convert_fusion = bf16[32,1024,512]{1,2,0:T(8,128)(2,1)} fusion(bf16[32,130,512]{2,0,1:T(8,128)(2,1)} %all-gather.15.cloned.1.call-done, f32[32,130,1024]{2,1,0:T(8,128)} %fusion.25, f32[32,1024]{1,0:T(8,128)S(1)} %copy-done.36), kind=kOutput, calls=%fused_computation.9 | convolution fusion | flops 4421451776 | bytes 54984704 | tf_op jit(solution)/shard_map/ecf,ecd->efd/dot_general | solution.py:134
  912.0 18.8 convolution_convert_fusion.1
  932.6 1.8 fusion.73
  934.7 3.2 fusion.66
  940.5 3.9 bitcast_reduce_fusion
  945.3 1.8 fusion.89
  947.2 56.0 %all-reduce.12 = (f32[512]{0:T(512)S(1)}, f32[512]{0:T(512)S(1)}, f32[512]{0:T(512)S(1)}, f32[512]{0:T(512)S(1)}, f32[512]{0:T(512)S(1)}) all-reduce(f32[512]{0:T(512)S(1)} %get-tuple-element.130, f32[512]{0:T(512)S(1)} %get-tuple-element.133, ...), channel_id=4, replica_groups=mesh['dp'=16,'tensor'=2] {'dp','tensor'}, use_global_device_ids=true, to_apply=%region_22.23.clone | all-reduce | flops 2560 | bytes 20480
  1006.1 26.5 %all-reduce.17.cloned.1.call-done = f32[3,512,512]{2,0,1:T(4,128)} async-done(((f32[3,512,512]{2,0,1:T(4,128)}), f32[3,512,512]{2,0,1:T(4,128)}) %all-reduce.17.cloned.1.call-update) | async-done | bytes 3145744
  1034.2 333.1 %reduce-scatter.20.cloned.1.call-done = bf16[32,1024,32]{1,2,0:T(8,128)(2,1)} async-done(((bf16[32,1024,512]{1,2,0:T(8,128)(2,1)}), bf16[32,1024,32]{1,2,0:T(8,128)(2,1)}) %reduce-scatter.20.cloned.1.call-update) | async-done | bytes 2097168 | tf_op jit(solution)/shard_map/reduce_scatter | solution.py:152
  1367.3 4.1 convert_element_type.207
  1371.4 329.9 %reduce-scatter.18.cloned.1.call-done = bf16[32,32,1024]{2,1,0:T(8,128)(2,1)} async-done(((bf16[32,512,1024]{2,1,0:T(8,128)(2,1)}), bf16[32,32,1024]{2,1,0:T(8,128)(2,1)}) %reduce-scatter.18.cloned.1.call-update) | async-done | bytes 2097168 | tf_op jit(solution)/shard_map/reduce_scatter | solution.py:146
  1701.3 4.1 convert_element_type.204
  1705.4 111.4 %reduce-scatter.22.cloned.1.call-done = f32[16,32]{1,0:T(8,128)} async-done(((f32[512,32]{1,0:T(8,128)}), f32[16,32]{1,0:T(8,128)}) %reduce-scatter.22.cloned.1.call-update) | async-done | bytes 2064
  1816.8 134.3 %reduce-scatter.16.cloned.1.call-done = f32[16,32]{1,0:T(8,128)} async-done(((f32[512,32]{1,0:T(8,128)}), f32[16,32]{1,0:T(8,128)}) %reduce-scatter.16.cloned.1.call-update) | async-done | bytes 2064 | tf_op jit(solution)/shard_map/reduce_scatter | solution.py:219
  1951.1 135.4 %reduce-scatter.14.cloned.1.call-done = f32[16,512]{1,0:T(8,128)} async-done(((f32[512,512]{1,0:T(8,128)}), f32[16,512]{1,0:T(8,128)}) %reduce-scatter.14.cloned.1.call-update) | async-done | bytes 32784 | tf_op jit(solution)/shard_map/reduce_scatter | solution.py:222
  (271 shorter events, 55.7 us)
Async XLA Ops:
  7.2 111.0 %all-gather.7.cloned.1.call-start = ((), (), s32[]{:S(2)}) async-start(), calls=%async_computation.7 | async-start | bytes 1622016 | tf_op jit(solution)/shard_map/all_gather | solution.py:46
  8.8 284.8 %all-gather.9.cloned.1.call-start = ((), (), s32[]{:S(2)}) async-start(), calls=%async_computation.8 | async-start | bytes 6389760 | tf_op jit(solution)/shard_map/all_gather | solution.py:108
  52.9 68.5 %copy-start.58 = (f32[512]{0:T(512)}, f32[512]{0:T(512)S(1)}, u32[]{:S(2)}) copy-start(f32[512]{0:T(512)S(1)} %convert_element_type.160) | copy-start | bytes 6148
  52.9 68.5 %copy-start.63 = (f32[512]{0:T(512)}, f32[512]{0:T(512)S(1)}, u32[]{:S(2)}) copy-start(f32[512]{0:T(512)S(1)} %convert_element_type.162) | copy-start | bytes 6148
  53.7 89.8 %copy-start.55 = (f32[512]{0:T(512)}, f32[512]{0:T(512)S(1)}, u32[]{:S(2)}) copy-start(f32[512]{0:T(512)S(1)} %convert_element_type.174) | copy-start | bytes 6148
  59.4 62.0 %copy-start.41 = (f32[784]{0:T(1024)}, f32[784]{0:T(1024)S(1)}, u32[]{:S(2)}) copy-start(f32[784]{0:T(1024)S(1)} %broadcast_multiply_fusion.1) | copy-start | bytes 9412
  60.9 60.4 %copy-start.49 = (f32[784]{0:T(1024)}, f32[784]{0:T(1024)S(1)}, u32[]{:S(2)}) copy-start(f32[784]{0:T(1024)S(1)} %fusion.46) | copy-start | bytes 9412
  61.0 60.4 %copy-start.47 = (f32[784]{0:T(1024)}, f32[784]{0:T(1024)S(1)}, u32[]{:S(2)}) copy-start(f32[784]{0:T(1024)S(1)} %fusion.77) | copy-start | bytes 9412
  124.3 5.0 copy-start.16
  129.3 4.1 copy-start.22
  133.4 6.6 copy-start.31
  135.3 4.7 copy-start.11
  135.3 6.3 copy-start.9
  135.3 6.3 copy-start.29
  144.1 116.8 %copy-start.4 = (bf16[784,512]{1,0:T(8,128)(2,1)}, bf16[784,512]{1,0:T(8,128)(2,1)S(1)}, u32[]{:S(2)}) copy-start(bf16[784,512]{1,0:T(8,128)(2,1)S(1)} %add_convert_fusion.1) | copy-start | bytes 2408452
  156.0 241.4 %all-gather.11.cloned.1.call-start = ((), (), s32[]{:S(2)}) async-start(), calls=%async_computation.9 | async-start | bytes 35651584 | tf_op jit(solution)/shard_map/all_gather | solution.py:59
  160.3 4.1 copy-start.60
  160.3 38.7 %copy-start.61 = (f32[16,32]{1,0:T(8,128)S(1)}, f32[16,32]{1,0:T(8,128)}, u32[]{:S(2)}) copy-start(f32[16,32]{1,0:T(8,128)} %param.25) | copy-start | bytes 6148
  160.3 38.7 %copy-start.38 = (s32[784,2]{0,1:T(2,128)S(1)}, s32[784,2]{0,1:T(2,128)}, u32[]{:S(2)}) copy-start(s32[784,2]{0,1:T(2,128)} %param.30) | copy-start | bytes 18820
  160.3 39.1 %copy-start.19 = (bf16[784,512]{1,0:T(8,128)(2,1)S(1)}, bf16[784,512]{1,0:T(8,128)(2,1)}, u32[]{:S(2)}) copy-start(bf16[784,512]{1,0:T(8,128)(2,1)} %param.17) | copy-start | bytes 2408452
  160.3 406.9 %all-gather.13.cloned.1.call-start = ((), (), s32[]{:S(2)}) async-start(), calls=%async_computation.10 | async-start | bytes 35651584 | tf_op jit(solution)/shard_map/all_gather | solution.py:61
  164.4 462.1 %all-gather.15.cloned.1.call-start = ((), (), s32[]{:S(2)}) async-start(), calls=%async_computation.12 | async-start | bytes 6389760 | tf_op jit(solution)/shard_map/all_gather | solution.py:130
  199.6 6.9 copy-start.2
  260.9 13.2 copy-start.26
  261.3 12.9 copy-start.24
  261.3 12.9 copy-start.43
  261.4 12.8 copy-start.53
  261.4 12.8 copy-start
  261.4 13.3 copy-start.37
  293.5 273.7 %copy-start.35 = (f32[32,1024]{1,0:T(8,128)S(1)}, f32[32,1024]{1,0:T(8,128)}, u32[]{:S(2)}) copy-start(f32[32,1024]{1,0:T(8,128)} %reshape.311) | copy-start | bytes 393220
  293.5 443.1 %reduce-scatter.10.cloned.1.call-start = ((), (), s32[]{:S(2)}) async-start(), calls=%async_computation.11 | async-start | bytes 6389760 | tf_op jit(solution)/shard_map/reduce_scatter | solution.py:115
  597.3 176.7 %reduce-scatter.12.cloned.1.call-start = ((), (), s32[]{:S(2)}) async-start(), calls=%async_computation.13 | async-start | bytes 6389760 | tf_op jit(solution)/shard_map/reduce_scatter | solution.py:142
  683.8 51.2 %copy-start.57 = (s32[784,2]{0,1:T(2,128)S(1)}, s32[784,2]{0,1:T(2,128)}, u32[]{:S(2)}) copy-start(s32[784,2]{0,1:T(2,128)} %get-tuple-element.147) | copy-start | bytes 18820
  683.8 255.4 %all-reduce.19.cloned.1.call-start = ((), (), s32[]{:S(2)}) async-start(), calls=%async_computation.20 | async-start | bytes 131072
  736.4 296.2 %all-reduce.17.cloned.1.call-start = ((), (), s32[]{:S(2)}) async-start(), calls=%async_computation.19 | async-start | bytes 8388608
  757.2 5.3 copy-start.3
  762.5 11.4 copy-start.25
  762.5 11.4 copy-start.44
  762.5 11.4 copy-start.54
  796.5 18.3 copy-start.1
  796.5 18.3 copy-start.8
  796.5 18.3 copy-start.27
  796.5 18.3 copy-start.40
  796.5 18.3 copy-start.46
  796.5 18.3 copy-start.56
  796.6 19.8 copy-start.52
  796.6 19.9 copy-start.13
  821.6 4.3 copy-start.12
  829.7 11.8 copy-start.18
  860.9 6.3 copy-start.23
  863.1 5.7 copy-start.10
  863.1 5.7 copy-start.42
  863.1 5.7 copy-start.48
  863.1 5.7 copy-start.59
  863.1 5.7 copy-start.64
  872.4 5.2 copy-start.36
  877.6 489.7 %reduce-scatter.20.cloned.1.call-start = ((), (), s32[]{:S(2)}) async-start(), calls=%async_computation.17 | async-start | bytes 35651584 | tf_op jit(solution)/shard_map/reduce_scatter | solution.py:152
  912.0 789.3 %reduce-scatter.18.cloned.1.call-start = ((), (), s32[]{:S(2)}) async-start(), calls=%async_computation.16 | async-start | bytes 35651584 | tf_op jit(solution)/shard_map/reduce_scatter | solution.py:146
  930.9 7.1 copy-start.65
  930.9 885.9 %reduce-scatter.22.cloned.1.call-start = ((), (), s32[]{:S(2)}) async-start(), calls=%async_computation.18 | async-start | bytes 270336
  932.5 1018.6 %reduce-scatter.16.cloned.1.call-start = ((), (), s32[]{:S(2)}) async-start(), calls=%async_computation.15 | async-start | bytes 270336 | tf_op jit(solution)/shard_map/reduce_scatter | solution.py:219
  934.4 1152.1 %reduce-scatter.14.cloned.1.call-start = ((), (), s32[]{:S(2)}) async-start(), calls=%async_computation.14 | async-start | bytes 1081344 | tf_op jit(solution)/shard_map/reduce_scatter | solution.py:222
  940.5 3.9 copy-start.50
  940.5 4.8 copy-start.21
  (16 other events, 30.3 us)
Sparse Core Ops, SparseCore 0:
  11.6 55.7 all-gather.6
  156.1 71.3 all-gather.8
  229.1 168.2 all-gather.10
  398.8 168.3 all-gather.12
  569.2 57.2 all-gather.14
  628.6 55.0 reduce-scatter.9
  686.1 57.5 reduce-scatter.11
  747.1 88.6 all-reduce.18
  877.7 154.8 all-reduce.16
  1036.7 330.5 reduce-scatter.19
  1371.5 329.7 reduce-scatter.17
  1704.0 112.7 reduce-scatter.21
  1819.6 131.4 reduce-scatter.15
  1953.8 132.6 reduce-scatter.13
where the time goes:
time: 2120 us; the launch traced here: 2090 us
  waiting for transfers between devices  1350 us (64%)
  blocking collectives  287 us (14%)
  matrix products  211 us (10%)
  local copies, waits for them, and re-layouts  152 us (7%)
  other arithmetic  76.2 us (4%)
    reduce_scatter x1, waiting for transfers between devices, per_device(): lax.psum_scatter(grad_second.astype(jnp.bfloat16), 'dp', scatter_dimensio...  333 us
    reduce_scatter x1, waiting for transfers between devices, per_device(): lax.psum_scatter(grad_first_w.astype(jnp.bfloat16), 'dp', scatter_dimensi...  330 us
    all_gather x1, waiting for transfers between devices, per_device(): lax.all_gather(w_back.astype(low_type), 'dp', axis=2, tiled=True)  146 us
    unnamed x17, waiting for transfers between devices  138 us
    reduce_scatter x1, waiting for transfers between devices, per_device(): lax.psum_scatter(grad_out_w, ('dp', 'tensor'), scatter_dimension=0, tiled...  135 us
    reduce_scatter x1, waiting for transfers between devices, per_device(): lax.psum_scatter(grad_router, ('dp', 'tensor'), scatter_dimension=0, tile...  134 us
    all_gather x1, waiting for transfers between devices, per_device(): lax.all_gather(w_in.astype(low_type), 'dp', axis=1, tiled=True)  104 us
    unnamed x2, blocking collectives  95.7 us
  transfers between devices with their start and end apart: 14, of which 9 were waited for; matrix products, arithmetic and copies ran while one was open for 19% of the time, Pallas kernels for 0%

commit v1 on v0

v1 whole, which is shorter than its diff:
```python
import jax
import jax.numpy as jnp
from jax import lax
from jax.sharding import PartitionSpec as P

H = 8
HD = 64
SEQ = 196
CAP = 65
LOW = jnp.bfloat16
WIDE = jnp.float32


def norm_affine(values_in, gain_vec, shift_vec):
    center = values_in - jnp.mean(values_in, axis=-1, keepdims=True)
    spread = jnp.mean(center * center, axis=-1, keepdims=True)
    return center * lax.rsqrt(spread + 1e-06) * gain_vec + shift_vec


def make_per_device(dp, tn):
    everyone = ("dp", "tensor")
    n = dp * tn

    def per_device(
        tokens,
        cotangent,
        ln1_scale,
        ln1_shift,
        w_qkv,
        w_out,
        out_bias,
        ln2_scale,
        ln2_shift,
        w_router,
        w_in,
        b_in,
        w_back,
        b_back,
        choices,
        slots,
    ):
        rows_here, width = tokens.shape
        images = rows_here // SEQ
        experts, blk_d, blk_f = w_in.shape
        ff = blk_f * tn
        dense_blk = w_out.shape[0]
        whole = experts % n == 0
        owners = n if whole else dp
        owned = experts // owners
        expert_axes = ("tensor", "dp") if whole else ("dp",)
        slot_total = experts * CAP
        score_scale = HD ** (-0.5)

        w_pack = jnp.stack([w_in.astype(LOW), jnp.swapaxes(w_back, 1, 2).astype(LOW)], axis=1)
        w_all = lax.all_to_all(w_pack, expert_axes, split_axis=0, concat_axis=0, tiled=True)
        f_parts = tn if whole else 1
        w_all = w_all.reshape(f_parts, dp, owned, 2, blk_d, blk_f)
        w_all = w_all.transpose(3, 2, 1, 4, 0, 5).reshape(2, owned, width, f_parts * blk_f)
        first_w, second_wt = w_all[0], w_all[1]

        vec_rows = jnp.stack([ln1_scale, ln1_shift, out_bias, ln2_scale, ln2_shift])
        pieces = [
            w_qkv.reshape(-1),
            w_out.reshape(-1),
            w_router.reshape(-1),
            b_back.reshape(-1),
            b_in.reshape(-1),
            vec_rows.reshape(-1),
        ]
        sizes = [p.shape[0] for p in pieces]
        total = sum(sizes)
        pad = -total % 512
        packed = jnp.concatenate([p.astype(LOW) for p in pieces] + [jnp.zeros((pad,), LOW)])
        gathered = lax.all_gather(packed.reshape(-1, 512), everyone, axis=0, tiled=False)
        gathered = gathered.reshape(n, -1)
        offs = [sum(sizes[:i]) for i in range(len(sizes))]
        part = [gathered[:, o : o + s] for o, s in zip(offs, sizes)]
        qkv_w = part[0].reshape(n, 3, dense_blk, width).swapaxes(0, 1).reshape(3, width, width)
        out_w = part[1].reshape(width, width)
        router = part[2].reshape(width, experts)
        bias_back = part[3].reshape(n, experts, -1).swapaxes(0, 1).reshape(experts, width)
        bias_back = bias_back.astype(WIDE)
        in_b = part[4].reshape(dp, tn, experts // dp, blk_f).swapaxes(1, 2).reshape(experts, ff)
        vecs = part[5].reshape(n, 5, -1).swapaxes(0, 1).reshape(5, width).astype(WIDE)
        gain_one, shift_one, bias_attn, gain_two, shift_two = vecs
        if whole:
            mine = lax.axis_index("tensor") * dp + lax.axis_index("dp")
            my_b = lax.dynamic_slice(in_b, (mine * owned, 0), (owned, ff)).astype(WIDE)
        else:
            my_b = lax.dynamic_slice(
                in_b,
                (lax.axis_index("dp") * owned, lax.axis_index("tensor") * blk_f),
                (owned, blk_f),
            ).astype(WIDE)

        residual = tokens.astype(WIDE)
        normed_one = norm_affine(residual, gain_one, shift_one).astype(LOW)
        projected = jnp.einsum(
            "td,jde->jte", normed_one, qkv_w, preferred_element_type=WIDE
        ).astype(LOW)
        head_query = projected[0].reshape(images, SEQ, H, HD)
        head_key = projected[1].reshape(images, SEQ, H, HD)
        head_value = projected[2].reshape(images, SEQ, H, HD)
        raw_scores = jnp.einsum(
            "ishd,ithd->ihst", head_query, head_key, preferred_element_type=WIDE
        )
        scaled = raw_scores * score_scale
        row_top = jnp.max(scaled, axis=-1, keepdims=True)
        log_total = row_top + jnp.log(jnp.sum(jnp.exp(scaled - row_top), axis=-1, keepdims=True))
        weights_att = jnp.exp(scaled - log_total).astype(LOW)
        attended = (
            jnp.einsum("ihst,ithd->ishd", weights_att, head_value, preferred_element_type=WIDE)
            .astype(LOW)
            .reshape(rows_here, width)
        )
        attn_sum = jnp.dot(attended, out_w, preferred_element_type=WIDE)
        middle = residual + attn_sum + bias_attn
        normed_two = norm_affine(middle, gain_two, shift_two).astype(LOW)
        route_p = jax.nn.softmax(jnp.dot(normed_two, router, preferred_element_type=WIDE), axis=-1)

        expert_ids = jnp.arange(experts, dtype=jnp.int32)
        chosen = [
            (choices[:, k : k + 1] == expert_ids[None, :]).astype(WIDE) for k in range(2)
        ]
        gate_vals = jnp.concatenate(
            [jnp.sum(route_p * c, axis=1, keepdims=True) for c in chosen], axis=1
        )
        kept_pair = (slots >= 0).astype(WIDE)
        target = jnp.where(slots >= 0, choices * CAP + slots, -1)
        places = jnp.arange(slot_total, dtype=jnp.int32)
        by_slot = [target[:, k][None, :] == places[:, None] for k in range(2)]
        spread_mat = (by_slot[0] | by_slot[1]).astype(LOW)
        by_token = [target[:, k : k + 1] == places[None, :] for k in range(2)]
        pair_weight = gate_vals * kept_pair
        slot_gate = jnp.sum(
            jnp.where(by_slot[0], pair_weight[:, 0][None, :], 0.0)
            + jnp.where(by_slot[1], pair_weight[:, 1][None, :], 0.0),
            axis=1,
            keepdims=True,
        )
        both = jnp.dot(
            spread_mat,
            jnp.concatenate([normed_two, cotangent], axis=1),
            preferred_element_type=WIDE,
        )
        buffer = both[:, :width].astype(LOW).reshape(experts, CAP, width)
        slot_grad = slot_gate * both[:, width:]
        grad_bias_back = jnp.sum(slot_grad.reshape(experts, CAP, width), axis=1)
        slot_grad_low = slot_grad.astype(LOW).reshape(experts, CAP, width)

        def out_to_experts(rows):
            width_c = rows.shape[1]
            if not whole:
                rows = lax.all_gather(rows, "tensor", axis=1, tiled=True)
            rows = lax.all_to_all(rows, expert_axes, split_axis=0, concat_axis=0, tiled=True)
            return rows.reshape(owners, owned, -1, width)

        def back_to_tokens(rows):
            rows = rows.reshape(experts, -1, width)
            rows = lax.all_to_all(rows, expert_axes, split_axis=0, concat_axis=0, tiled=True)
            if not whole:
                rows = lax.psum_scatter(rows, "tensor", scatter_dimension=1, tiled=True)
            return rows

        sent = out_to_experts(jnp.concatenate([buffer, slot_grad_low], axis=1))
        group = sent.shape[2] // (2 * CAP)
        sent = sent.reshape(owners, owned, group, 2, CAP, width).transpose(3, 1, 0, 2, 4, 5)
        sent = sent.reshape(2, owned, owners * group * CAP, width)
        all_slots, slot_grad_all = sent[0], sent[1]

        pre_act = (
            jnp.einsum("ecd,edf->ecf", all_slots, first_w, preferred_element_type=WIDE)
            + my_b[:, None, :]
        )
        hidden, gelu_pull = jax.vjp(lambda member: jax.nn.gelu(member, approximate=True), pre_act)
        hidden = hidden.astype(LOW)
        expert_sum = jnp.einsum("ecf,edf->ecd", hidden, second_wt, preferred_element_type=WIDE)
        grad_hidden = jnp.einsum("ecd,edf->ecf", slot_grad_all, second_wt, preferred_element_type=WIDE)
        grad_pre = gelu_pull(grad_hidden)[0].astype(LOW)
        grad_slots_all = jnp.einsum("ecf,edf->ecd", grad_pre, first_w, preferred_element_type=WIDE)
        returned = jnp.stack([expert_sum.astype(LOW), grad_slots_all.astype(LOW)])
        returned = returned.reshape(2, owned, owners, group, CAP, width).transpose(2, 1, 3, 0, 4, 5)
        returned = returned.reshape(owners * owned, group * 2 * CAP, width)
        home = back_to_tokens(returned).reshape(experts, 2, CAP, width)
        expert_home = home[:, 0].reshape(slot_total, width)
        grad_home = home[:, 1].reshape(slot_total, width)

        grad_first_b = jnp.sum(grad_pre.astype(WIDE), axis=1)
        grad_first_w = jnp.einsum("ecd,ecf->edf", all_slots, grad_pre, preferred_element_type=WIDE)
        grad_second_t = jnp.einsum("ecd,ecf->edf", slot_grad_all, hidden, preferred_element_type=WIDE)
        g_pack = jnp.stack([grad_first_w.astype(LOW), grad_second_t.astype(LOW)])
        g_pack = g_pack.reshape(2, owned, dp, blk_d, f_parts, blk_f).transpose(4, 2, 1, 0, 3, 5)
        g_pack = g_pack.reshape(f_parts * dp * owned, 2, blk_d, blk_f)
        g_home = lax.all_to_all(g_pack, expert_axes, split_axis=0, concat_axis=0, tiled=True)
        g_home = g_home.reshape(experts, 2, blk_d, blk_f).astype(WIDE)
        grad_w_in = g_home[:, 0]
        grad_w_back = jnp.swapaxes(g_home[:, 1], 1, 2)

        picked = []
        for k in range(2):
            rows = jnp.dot(by_token[k].astype(LOW), expert_home, preferred_element_type=WIDE)
            bias_rows = jnp.dot(
                chosen[k].astype(LOW), bias_back.astype(LOW), preferred_element_type=WIDE
            )
            picked.append((rows + bias_rows) * kept_pair[:, k : k + 1])
        result = (
            middle + gate_vals[:, 0:1] * picked[0] + gate_vals[:, 1:2] * picked[1]
        ).astype(LOW)
        grad_out = cotangent.astype(WIDE)
        grad_probs = sum(
            jnp.sum(grad_out * picked[k], axis=1, keepdims=True) * chosen[k] for k in range(2)
        )
        gather_mat = (by_token[0] | by_token[1]).astype(LOW)
        grad_normed_two = jnp.dot(gather_mat, grad_home, preferred_element_type=WIDE)
        grad_logits = route_p * (grad_probs - jnp.sum(grad_probs * route_p, axis=-1, keepdims=True))
        grad_normed_two = grad_normed_two + jnp.dot(
            grad_logits, router.astype(WIDE).T, precision=lax.Precision.HIGHEST
        )
        grad_router = jnp.dot(
            normed_two.astype(WIDE).T, grad_logits, precision=lax.Precision.HIGHEST
        )
        _, pull_two = jax.vjp(norm_affine, middle, gain_two, shift_two)
        grad_mid_norm, grad_gain_two, grad_shift_two = pull_two(grad_normed_two)
        grad_middle = grad_out + grad_mid_norm
        grad_bias_attn = jnp.sum(grad_middle, axis=0)
        grad_mid_low = grad_middle.astype(LOW)
        grad_att = jnp.einsum(
            "td,ed->te", grad_mid_low, out_w, preferred_element_type=WIDE
        ).astype(LOW)
        grad_out_w = jnp.einsum("te,td->ed", attended, grad_mid_low, preferred_element_type=WIDE)
        grad_att_heads = grad_att.reshape(images, SEQ, H, HD)
        probs_again = jnp.exp(
            jnp.einsum("ishd,ithd->ihst", head_query, head_key, preferred_element_type=WIDE)
            * score_scale
            - log_total
        )
        grad_weights = jnp.einsum(
            "ishd,ithd->ihst", grad_att_heads, head_value, preferred_element_type=WIDE
        )
        row_delta = jnp.sum(grad_weights * probs_again, axis=-1, keepdims=True)
        grad_raw = (probs_again * (grad_weights - row_delta) * score_scale).astype(LOW)
        grad_value = jnp.einsum(
            "ihst,ishd->ithd",
            probs_again.astype(LOW),
            grad_att_heads,
            preferred_element_type=WIDE,
        )
        grad_query = jnp.einsum("ihst,ithd->ishd", grad_raw, head_key, preferred_element_type=WIDE)
        grad_key = jnp.einsum("ihst,ishd->ithd", grad_raw, head_query, preferred_element_type=WIDE)
        grad_proj = jnp.stack(
            [
                grad_query.astype(LOW).reshape(rows_here, width),
                grad_key.astype(LOW).reshape(rows_here, width),
                grad_value.astype(LOW).reshape(rows_here, width),
            ]
        )
        grad_qkv_w = jnp.einsum("td,jte->jde", normed_one, grad_proj, preferred_element_type=WIDE)
        grad_normed_one = jnp.einsum("jte,jde->td", grad_proj, qkv_w, preferred_element_type=WIDE)
        _, pull_one = jax.vjp(norm_affine, residual, gain_one, shift_one)
        grad_resid_norm, grad_gain_one, grad_shift_one = pull_one(grad_normed_one)
        grad_tokens = grad_middle + grad_resid_norm

        if whole:
            row_b = jnp.zeros((experts, ff), WIDE)
            row_b = lax.dynamic_update_slice(row_b, grad_first_b, (mine * owned, 0))
        else:
            row_b = jnp.zeros((experts, ff), WIDE)
            row_b = lax.dynamic_update_slice(
                row_b,
                grad_first_b,
                (lax.axis_index("dp") * owned, lax.axis_index("tensor") * blk_f),
            )
        vec_grads = jnp.stack(
            [grad_gain_one, grad_shift_one, grad_bias_attn, grad_gain_two, grad_shift_two]
        )
        out_pieces = [
            grad_qkv_w.reshape(3, n, dense_blk, width).swapaxes(0, 1).reshape(n, -1),
            grad_out_w.reshape(n, -1),
            grad_router.reshape(n, -1),
            grad_bias_back.reshape(experts, n, -1).swapaxes(0, 1).reshape(n, -1),
            row_b.reshape(dp, experts // dp, tn, blk_f).swapaxes(1, 2).reshape(n, -1),
            vec_grads.reshape(5, n, -1).swapaxes(0, 1).reshape(n, -1),
        ]
        out_pack = jnp.concatenate(
            [p.astype(LOW) for p in out_pieces] + [jnp.zeros((n, pad), LOW)], axis=1
        )
        out_all = lax.all_to_all(
            out_pack.reshape(n, -1, 512), everyone, split_axis=0, concat_axis=0, tiled=True
        )
        summed = jnp.sum(out_all.astype(WIDE), axis=0).reshape(-1)
        done = [summed[o : o + s] for o, s in zip(offs, sizes)]
        vec_done = done[5].reshape(5, -1)
        return (
            result,
            grad_tokens,
            vec_done[0],
            vec_done[1],
            done[0].reshape(w_qkv.shape),
            done[1].reshape(w_out.shape),
            vec_done[2],
            vec_done[3],
            vec_done[4],
            done[2].reshape(w_router.shape),
            grad_w_in,
            done[4].reshape(b_in.shape),
            grad_w_back,
            done[3].reshape(b_back.shape),
        )

    return per_device


def solution(mesh):
    everyone = ("dp", "tensor")
    in_specs = (
        P(everyone, None),
        P(everyone, None),
        P(everyone),
        P(everyone),
        P(None, everyone, None),
        P(everyone, None),
        P(everyone),
        P(everyone),
        P(everyone),
        P(everyone, None),
        P(None, "dp", "tensor"),
        P("dp", "tensor"),
        P(None, "tensor", "dp"),
        P(None, everyone),
        P(everyone, None),
        P(everyone, None),
    )
    out_specs = in_specs[:2] + in_specs[2:14]
    return jax.shard_map(
        make_per_device(mesh.shape["dp"], mesh.shape["tensor"]),
        mesh=mesh,
        in_specs=in_specs,
        out_specs=out_specs,
        check_vma=False,
    )
```

time: 2120 us -> 639 us (0.30)
  waiting for transfers between devices: 1350 us -> 238 us
  blocking collectives: 287 us -> 0 us
  matrix products: 211 us -> 129 us
  starting transfers between devices: 1.62 us -> 36.5 us
  other arithmetic: 76.2 us -> 45.1 us
    reduce_scatter x6 -> x0, waiting for transfers between devices: 933 us -> none  [the longest x1 333 us: per_device(): lax.psum_scatter(grad_second.astype(jnp.bfloat16), 'dp', scatter_dimensio...]
    all_gather x5 -> x1, waiting for transfers between devices: 279 us -> 64.6 us  [per_device(): lax.all_gather(packed.reshape(-1, 512), everyone, axis=0, tiled=False)]
    all_gather x4 -> x0, blocking collectives: 191 us -> none  [the longest x1 57.2 us: per_device(): lax.all_gather(w_out.astype(low_type), ('dp', 'tensor'), axis=0, tiled=True)]
    all_to_all x0 -> x5, waiting for transfers between devices: none -> 173 us  [the longest x1 81.6 us: out_to_experts(): lax.all_to_all(rows, expert_axes, split_axis=0, concat_axis=0, tiled=True)]
    unnamed x17 -> x1, waiting for transfers between devices: 138 us -> 0.02 us
    unnamed x2 -> x0, blocking collectives: 95.7 us -> none
    dot_general x16 -> x22, matrix products: 176 us -> 96.7 us  [the longest x1 17.1 us: per_device(): jnp.einsum('ecd,edf->ecf', slot_grad_all, second_wt, preferred_element_ty...]
    gather x14 -> x0, local copies, waits for them, and re-layouts: 73.1 us -> none  [the longest x2 13.8 us: per_device(): picked = expert_out[index_safe]]
  transfers between devices with their start and end apart: 14 -> 6, of which waited for: 9 -> 4; matrix products, arithmetic and copies ran while one was open for 19% -> 37% of each run, Pallas kernels for 0% -> 0%
where the time goes in v1:
time: 639 us; the launch traced here: 626 us
  waiting for transfers between devices  238 us (37%)
  local copies, waits for them, and re-layouts  151 us (24%)
  matrix products  129 us (20%)
  other arithmetic  45.1 us (7%)
  starting transfers between devices  36.5 us (6%)
  between operations  26.8 us (4%)
    all_to_all x1, waiting for transfers between devices, out_to_experts(): lax.all_to_all(rows, expert_axes, split_axis=0, concat_axis=0, tiled=True)  81.6 us
    all_gather x1, waiting for transfers between devices, per_device(): lax.all_gather(packed.reshape(-1, 512), everyone, axis=0, tiled=False)  64.6 us
    all_to_all x1, waiting for transfers between devices, back_to_tokens(): lax.all_to_all(rows, expert_axes, split_axis=0, concat_axis=0, tiled=True)  48.1 us
    all_to_all x1, waiting for transfers between devices, per_device(): lax.all_to_all(out_pack.reshape(n, -1, 512), everyone, split_axis=0, conc...  43.8 us
    unnamed x193, local copies, waits for them, and re-layouts  23.5 us
    dot_general x1, matrix products, per_device(): jnp.einsum('ecd,edf->ecf', slot_grad_all, second_wt, preferred_element_ty...  17.1 us
    dot_general x1, matrix products, per_device(): jnp.einsum('ecd,edf->ecf', all_slots, first_w, preferred_element_type=WIDE)  14.2 us
  transfers between devices with their start and end apart: 6, of which 4 were waited for; matrix products, arithmetic and copies ran while one was open for 37% of the time, Pallas kernels for 0%

profile of v1, /device:TPU:13, one launch (start us, length us, event | category | flops | bytes accessed | tf_op | source)
XLA Modules:
  0.0 626.1 jit_solution(60068635833417820)
XLA Ops:
  14.3 2.7 convert_bitcast_fusion.2
  18.1 2.4 pad_maximum_fusion.1
  20.5 6.3 %all-to-all-start.1 = ((bf16[32,2,32,1024]{3,2,1,0:T(8,128)(2,1)}), bf16[32,2,32,1024]{3,2,1,0:T(8,128)(2,1)}, u32[]{:S(2)}, u32[]{:S(2)}) async-start(bf16[32,2,32,1024]{3,2,1,0:T(8,128)(2,1)} %pad_maximum_fusion.1), calls=%async_computation.1 | async-start | bytes 8388608 | tf_op jit(solution)/shard_map/all_to_all | solution.py:55
  27.6 64.6 %all-gather.2.cloned.1.call-done = bf16[32,71,512]{2,1,0:T(8,128)(2,1)} async-done(((bf16[1,71,512]{2,1,0:T(8,128)(2,1)}), bf16[32,71,512]{2,1,0:T(8,128)(2,1)}) %all-gather.2.cloned.1.call-update) | async-done | bytes 2326544 | tf_op jit(solution)/shard_map/all_gather | solution.py:74
  92.2 2.5 copy.220
  99.2 2.1 reshape.365
  106.2 2.5 reshape.398
  113.2 2.5 reshape.396
  116.9 3.0 multiply_reduce_fusion.1
  128.6 4.9 fusion.12
  146.1 2.5 add_reduce_fusion
  148.6 3.2 fusion.113
  151.8 2.7 reshape.368
  154.5 4.1 reshape.367
  158.6 5.0 pad_maximum_fusion
  163.6 8.0 %all-to-all-start = ((bf16[32,130,512]{2,1,0:T(8,128)(2,1)}), bf16[32,130,512]{2,1,0:T(8,128)(2,1)}, u32[]{:S(2)}, u32[]{:S(2)}) async-start(bf16[32,130,512]{2,1,0:T(8,128)(2,1)} %pad_maximum_fusion), calls=%async_computation | async-start | bytes 8912896 | tf_op jit(solution)/shard_map/all_to_all | solution.py:155
  172.7 6.5 %copy.229 = bf16[2,16,1,2,32,1024]{5,0,4,1,2,3:T(2,128)(2,1)S(1)} copy(bf16[2,16,1,2,32,1024]{5,4,3,1,0,2:T(8,128)(2,1)} %bitcast.18) | data formatting | bytes 8388608 | tf_op jit(solution)/shard_map/reshape | solution.py:57
  179.2 3.0 fusion.116
  186.1 81.6 %all-to-all-done = bf16[32,130,512]{2,1,0:T(8,128)(2,1)} async-done(((bf16[32,130,512]{2,1,0:T(8,128)(2,1)}), bf16[32,130,512]{2,1,0:T(8,128)(2,1)}, u32[]{:S(2)}, u32[]{:S(2)}) %all-to-all-start) | async-done | bytes 4259872 | tf_op jit(solution)/shard_map/all_to_all | solution.py:155
  267.7 3.7 copy.162
  274.4 2.1 reshape.369
  276.5 2.8 copy.166
  279.3 2.2 reshape.375
  281.5 14.2 %multiply_convert_fusion = (bf16[2080,2048]{1,0:T(8,128)(2,1)S(1)}, f32[2080,2048]{1,0:T(8,128)}) fusion(f32[2048]{0:T(1024)S(1)} %bitcast.213, bf16[2080,512]{1,0:T(8,128)(2,1)} %reshape.369, bf16[512,2048]{1,0:T(8,128)(2,1)} %bitcast.187), kind=kOutput, calls=%fused_computation.11 | convolution fusion | flops 4404674560 | bytes 29794304 | tf_op jit(solution)/shard_map/ecd,edf->ecf/dot_general | solution.py:172
  295.7 6.2 convolution_convert_fusion.1
  301.9 17.1 %convert_reduce_fusion = (f32[2048]{0:T(1024)S(1)}, bf16[2080,2048]{1,0:T(8,128)(2,1)S(1)}) fusion(f32[2080,2048]{1,0:T(8,128)} %get-tuple-element.114, f32[2048]{0:T(1024)S(1)} %bitcast.214, bf16[2080,512]{1,0:T(8,128)(2,1)S(1)} %copy-done.23, bf16[512,2048]{1,0:T(8,128)(2,1)S(1)} %bitcast.190), kind=kOutput, calls=%fused_computation.10 | convolution fusion | flops 4460050432 | bytes 29802496 | tf_op jit(solution)/shard_map/ecd,edf->ecf/dot_general | solution.py:178
  319.0 3.3 copy-done.84
  322.2 6.1 convolution_convert_fusion
  328.3 2.7 stack.82
  331.0 4.3 stack.81
  335.3 2.1 maximum_bitcast_fusion
  339.0 4.4 copy.168
  343.5 7.9 %all-to-all-start.2 = ((bf16[32,130,512]{2,1,0:T(8,128)(2,1)}), bf16[32,130,512]{2,1,0:T(8,128)(2,1)}, u32[]{:S(2)}, u32[]{:S(2)}) async-start(bf16[32,130,512]{2,1,0:T(8,128)(2,1)} %copy.168), calls=%async_computation.2 | async-start | bytes 8912896 | tf_op jit(solution)/shard_map/all_to_all | solution.py:160
  351.7 5.1 reshape.381
  356.8 3.2 reduce_sum.252
  361.4 9.7 %convolution_convert_fusion.3 = bf16[512,2048]{1,0:T(8,128)(2,1)} fusion(bf16[2080,512]{1,0:T(8,128)(2,1)S(1)} %copy-done.22, bf16[2080,2048]{1,0:T(8,128)(2,1)} %copy-done.84), kind=kOutput, calls=%fused_computation.55 | convolution fusion | flops 4363124736 | bytes 12746752 | tf_op jit(solution)/shard_map/ecd,ecf->edf/dot_general | solution.py:189
  371.1 3.3 stack.91
  374.4 9.1 %convolution_convert_fusion.2 = bf16[512,2048]{1,0:T(8,128)(2,1)} fusion(bf16[2080,512]{1,0:T(8,128)(2,1)} %reshape.375, bf16[2080,2048]{1,0:T(8,128)(2,1)} %copy-done.83), kind=kOutput, calls=%fused_computation.54 | convolution fusion | flops 4363124736 | bytes 12746752 | tf_op jit(solution)/shard_map/ecd,ecf->edf/dot_general | solution.py:190
  383.5 4.7 stack.92
  388.2 7.9 %maximum_bitcast_fusion.1 = bf16[2,16,1,2,32,1024]{5,0,4,1,2,3:T(2,128)(2,1)S(1)} fusion(bf16[1,1,16,32,2,1024]{5,4,3,2,1,0:T(2,128)(2,1)} %stack.92, bf16[1,1,16,32,2,1024]{5,4,3,2,1,0:T(2,128)(2,1)S(1)} %stack.91), kind=kLoop, calls=%fused_computation.42 | loop fusion | flops 2097152 | bytes 8388608 | tf_op jit(solution)/shard_map/transpose | solution.py:192
  396.1 3.4 copy.197
  399.5 48.1 %all-to-all-done.2 = bf16[32,130,512]{2,1,0:T(8,128)(2,1)} async-done(((bf16[32,130,512]{2,1,0:T(8,128)(2,1)}), bf16[32,130,512]{2,1,0:T(8,128)(2,1)}, u32[]{:S(2)}, u32[]{:S(2)}) %all-to-all-start.2) | async-done | bytes 4259872 | tf_op jit(solution)/shard_map/all_to_all | solution.py:160
  447.5 8.3 %all-to-all-start.4 = ((bf16[32,2,32,1024]{3,2,1,0:T(8,128)(2,1)}), bf16[32,2,32,1024]{3,2,1,0:T(8,128)(2,1)}, u32[]{:S(2)}, u32[]{:S(2)}) async-start(bf16[32,2,32,1024]{3,2,1,0:T(8,128)(2,1)} %bitcast.173), calls=%async_computation.4 | async-start | bytes 8388608 | tf_op jit(solution)/shard_map/all_to_all | solution.py:194
  455.9 3.7 copy.169
  462.5 2.2 reshape_squeeze.18
  464.7 5.0 fusion.9
  469.7 3.3 fusion.11
  474.1 2.3 reshape_squeeze.19
  476.5 3.8 fusion.14
  482.0 2.0 fusion.52
  491.0 2.0 copy.175
  493.1 4.3 fusion.64
  502.5 3.5 reshape.395
  506.0 3.8 fusion.123
  509.8 11.6 %fusion.65 = bf16[4,196,8,64]{1,3,2,0:T(8,128)(2,1)} fusion(bf16[4,196,8,64]{1,3,2,0:T(8,128)(2,1)S(1)} %copy-done.13, f32[4,8,196,196]{2,3,1,0:T(8,128)} %fusion.123, f32[4,8,196,196]{2,3,1,0:T(8,128)} %copy-done, f32[4,8,196]{2,1,0:T(8,128)S(1)} %copy-done.41), kind=kOutput, calls=%fused_computation.103 | convolution fusion | flops 168823616 | bytes 11465216 | tf_op jit(solution)/shard_map/ihst,ishd->ithd/dot_general | solution.py:249
  521.4 2.1 copy.204
  524.6 12.6 %fusion.68 = bf16[4,196,8,64]{1,3,2,0:T(8,128)(2,1)} fusion(bf16[4,196,8,64]{1,3,2,0:T(8,128)(2,1)S(1)} %copy-done.12, f32[4,8,196,196]{2,3,1,0:T(8,128)} %fusion.123, f32[4,8,196,196]{2,3,1,0:T(8,128)} %copy-done, f32[4,8,196]{2,1,0:T(8,128)S(1)} %copy-done.41), kind=kOutput, calls=%fused_computation.104 | convolution fusion | flops 168823616 | bytes 11465216 | tf_op jit(solution)/shard_map/ihst,ithd->ishd/dot_general | solution.py:248
  537.2 2.1 copy.203
  549.8 2.1 fusion.111
  554.8 2.6 reshape.382
  557.4 5.9 all-to-all-start.3
  563.3 3.2 convert_element_type.301
  566.6 4.2 slice_bitcast_fusion
  570.8 43.8 %all-to-all-done.3 = bf16[32,71,512]{2,1,0:T(8,128)(2,1)S(1)} async-done(((bf16[32,71,512]{2,1,0:T(8,128)(2,1)}), bf16[32,71,512]{2,1,0:T(8,128)(2,1)S(1)}, u32[]{:S(2)}, u32[]{:S(2)}) %all-to-all-start.3) | async-done | bytes 2326560 | tf_op jit(solution)/shard_map/all_to_all | solution.py:287
  (325 shorter events, 81.6 us)
Async XLA Ops:
  7.2 85.0 %all-gather.2.cloned.1.call-start = ((), (), s32[]{:S(2)}) async-start(), calls=%async_computation.5 | async-start | bytes 2433024 | tf_op jit(solution)/shard_map/all_gather | solution.py:74
  14.3 3.5 copy-start.11
  20.4 6.3 %copy-start.72 = (s32[784,2]{0,1:T(2,128)S(1)}, s32[784,2]{0,1:T(2,128)}, u32[]{:S(2)}) copy-start(s32[784,2]{0,1:T(2,128)} %param.30) | copy-start | bytes 18820
  20.5 6.4 %copy-start.3 = (bf16[784,512]{1,0:T(8,128)(2,1)S(1)}, bf16[784,512]{1,0:T(8,128)(2,1)}, u32[]{:S(2)}) copy-start(bf16[784,512]{1,0:T(8,128)(2,1)} %param.16) | copy-start | bytes 2408452
  20.5 6.6 %copy-start.57 = (s32[784,2]{0,1:T(2,128)S(1)}, s32[784,2]{0,1:T(2,128)}, u32[]{:S(2)}) copy-start(s32[784,2]{0,1:T(2,128)} %param.31) | copy-start | bytes 18820
  20.5 143.1 %all-to-all-start.1 = ((bf16[32,2,32,1024]{3,2,1,0:T(8,128)(2,1)}), bf16[32,2,32,1024]{3,2,1,0:T(8,128)(2,1)}, u32[]{:S(2)}, u32[]{:S(2)}) async-start(bf16[32,2,32,1024]{3,2,1,0:T(8,128)(2,1)} %pad_maximum_fusion.1), calls=%async_computation.1 | async-start | bytes 8388608 | tf_op jit(solution)/shard_map/all_to_all | solution.py:55
  26.8 101.2 %copy-start.45 = (s32[784]{0:T(1024)}, s32[784]{0:T(1024)S(1)}, u32[]{:S(2)}) copy-start(s32[784]{0:T(1024)S(1)} %get-tuple-element.73) | copy-start | bytes 9412
  26.9 101.2 %copy-start.47 = (s32[784]{0:T(1024)}, s32[784]{0:T(1024)S(1)}, u32[]{:S(2)}) copy-start(s32[784]{0:T(1024)S(1)} %get-tuple-element.74) | copy-start | bytes 9412
  27.1 108.2 %copy-start.77 = (s32[784]{0:T(1024)}, s32[784]{0:T(1024)S(1)}, u32[]{:S(2)}) copy-start(s32[784]{0:T(1024)S(1)} %get-tuple-element.75) | copy-start | bytes 9412
  27.1 118.9 %copy-start.79 = (s32[784]{0:T(1024)}, s32[784]{0:T(1024)S(1)}, u32[]{:S(2)}) copy-start(s32[784]{0:T(1024)S(1)} %get-tuple-element.76) | copy-start | bytes 9412
  27.2 76.2 %copy-start.51 = (f32[784]{0:T(1024)}, f32[784]{0:T(1024)S(1)}, u32[]{:S(2)}) copy-start(f32[784]{0:T(1024)S(1)} %broadcast_multiply_fusion.1) | copy-start | bytes 9412
  27.6 67.1 %copy-start.58 = (f32[784]{0:T(1024)}, f32[784]{0:T(1024)S(1)}, u32[]{:S(2)}) copy-start(f32[784]{0:T(1024)S(1)} %fusion.49) | copy-start | bytes 9412
  27.6 75.7 %copy-start.66 = (f32[784]{0:T(1024)}, f32[784]{0:T(1024)S(1)}, u32[]{:S(2)}) copy-start(f32[784]{0:T(1024)S(1)} %fusion.94) | copy-start | bytes 9412
  94.7 3.7 copy-start.7
  97.1 29.9 %copy-start.68 = (f32[512]{0:T(512)}, f32[512]{0:T(512)S(1)}, u32[]{:S(2)}) copy-start(f32[512]{0:T(512)S(1)} %mul.290) | copy-start | bytes 6148
  97.6 5.7 copy-start.81
  97.8 5.6 copy-start.73
  116.9 4.4 copy-start.5
  120.0 2.8 copy-start
  126.6 2.0 copy-start.14
  127.0 6.6 %copy-start.60 = (f32[784]{0:T(1024)}, f32[784]{0:T(1024)S(1)}, u32[]{:S(2)}) copy-start(f32[784]{0:T(1024)S(1)} %multiply_reduce_fusion.4) | copy-start | bytes 9412
  127.0 6.6 %copy-start.55 = (f32[784]{0:T(1024)}, f32[784]{0:T(1024)S(1)}, u32[]{:S(2)}) copy-start(f32[784]{0:T(1024)S(1)} %fusion.95) | copy-start | bytes 9412
  127.6 6.0 copy-start.17
  128.1 5.5 copy-start.62
  128.1 5.5 copy-start.64
  163.6 104.2 %all-to-all-start = ((bf16[32,130,512]{2,1,0:T(8,128)(2,1)}), bf16[32,130,512]{2,1,0:T(8,128)(2,1)}, u32[]{:S(2)}, u32[]{:S(2)}) async-start(bf16[32,130,512]{2,1,0:T(8,128)(2,1)} %pad_maximum_fusion), calls=%async_computation | async-start | bytes 8912896 | tf_op jit(solution)/shard_map/all_to_all | solution.py:155
  281.5 14.2 %copy-start.26 = (bf16[64,8,2,1024]{3,1,2,0:T(8,128)(2,1)S(1)}, bf16[64,8,2,1024]{3,1,2,0:T(8,128)(2,1)}, u32[]{:S(2)}) copy-start(bf16[64,8,2,1024]{3,1,2,0:T(8,128)(2,1)} %copy.224) | copy-start | bytes 6291460
  295.7 6.2 copy-start.83
  295.7 6.2 copy-start.23
  301.9 20.4 %copy-start.25 = (bf16[64,8,2,1024]{3,1,2,0:T(8,128)(2,1)S(1)}, bf16[64,8,2,1024]{3,1,2,0:T(8,128)(2,1)}, u32[]{:S(2)}) copy-start(bf16[64,8,2,1024]{3,1,2,0:T(8,128)(2,1)} %copy.222) | copy-start | bytes 6291460
  319.0 3.3 copy-start.84
  343.5 7.9 %copy-start.42 = (bf16[32,512]{1,0:T(8,128)(2,1)S(1)}, bf16[32,512]{1,0:T(8,128)(2,1)}, u32[]{:S(2)}) copy-start(bf16[32,512]{1,0:T(8,128)(2,1)} %get-tuple-element.95) | copy-start | bytes 98308
  343.5 104.1 %all-to-all-start.2 = ((bf16[32,130,512]{2,1,0:T(8,128)(2,1)}), bf16[32,130,512]{2,1,0:T(8,128)(2,1)}, u32[]{:S(2)}, u32[]{:S(2)}) async-start(bf16[32,130,512]{2,1,0:T(8,128)(2,1)} %copy.168), calls=%async_computation.2 | async-start | bytes 8912896 | tf_op jit(solution)/shard_map/all_to_all | solution.py:160
  356.8 4.6 copy-start.22
  447.5 109.9 %all-to-all-start.4 = ((bf16[32,2,32,1024]{3,2,1,0:T(8,128)(2,1)}), bf16[32,2,32,1024]{3,2,1,0:T(8,128)(2,1)}, u32[]{:S(2)}, u32[]{:S(2)}) async-start(bf16[32,2,32,1024]{3,2,1,0:T(8,128)(2,1)} %bitcast.173), calls=%async_computation.4 | async-start | bytes 8388608 | tf_op jit(solution)/shard_map/all_to_all | solution.py:194
  462.5 2.2 copy-start.80
  464.7 5.0 copy-start.24
  464.7 5.0 copy-start.78
  469.7 3.3 copy-start.8
  476.4 3.9 copy-start.28
  476.4 3.9 copy-start.48
  476.5 4.4 copy-start.29
  481.9 2.1 copy-start.21
  481.9 2.1 copy-start.44
  482.0 2.1 copy-start.54
  482.0 2.1 copy-start.33
  482.0 2.1 copy-start.50
  482.0 2.1 copy-start.56
  482.0 2.1 copy-start.69
  486.5 2.1 copy-start.9
  486.5 2.1 copy-start.37
  486.5 2.8 copy-start.75
  489.3 3.8 copy-start.41
  493.1 4.3 copy-start.18
  493.1 4.8 copy-start.38
  500.6 5.4 copy-start.6
  506.0 3.8 copy-start.13
  521.4 3.1 copy-start.12
  539.2 3.1 copy-start.19
  549.8 2.4 copy-start.70
  549.8 2.4 copy-start.71
  551.9 2.0 copy-start.27
  551.9 2.1 copy-start.39
  557.4 57.1 %all-to-all-start.3 = ((bf16[32,71,512]{2,1,0:T(8,128)(2,1)}), bf16[32,71,512]{2,1,0:T(8,128)(2,1)S(1)}, u32[]{:S(2)}, u32[]{:S(2)}) async-start(bf16[32,71,512]{2,1,0:T(8,128)(2,1)} %reshape.382), calls=%async_computation.3 | async-start | bytes 4718592 | tf_op jit(solution)/shard_map/all_to_all | solution.py:287
  (27 other events, 37.6 us)
Sparse Core Ops, SparseCore 0:
  14.4 77.7 all-gather.1
